TPU v7x, 32 devices: a whole 2x2x4 slice. The times are simulated.
32 devices in a mesh: member: 2 (over core), shard: 16 (over z, y, x).
Axes of the slice: x: 2, y: 2, z: 4, core: 2. Of those that a mesh axis runs over, the one named last changes fastest.
Arguments:
- layer_input: bfloat16 [2, 180, 5120], P('member', None, 'shard'), may hold values from -6 to 6
- norm_gain: float32 [2, 5120], P('member'), may hold values from 0.5 to 2
- w_gate: bfloat16 [2, 5120, 1792], P('member', None, 'shard'), may hold values from -0.0559017 to 0.0559017
- w_up: bfloat16 [2, 5120, 1792], P('member', None, 'shard'), may hold values from -0.0559017 to 0.0559017
- hidden_cot: bfloat16 [2, 180, 1792], P('member', None, 'shard'), may hold values from -3 to 5
- output_cot: bfloat16 [2, 180, 5120], P('member', None, 'shard'), may hold values from -6 to 6
- embed: bfloat16 [2, 4096, 5120], P('member', 'shard'), may hold values from -0.078125 to 0.078125
- suffix_ids: int32 [180], replicated, may hold values from 0 to 4095
Outputs:
- delta: float32 [180, 4096], P(None, 'shard')
All inputs are finite; a program needn't handle non-finite values.
Results may differ from a plain program's by a relative error of at most 0.0047.
Values may be sent and summed in bfloat16 or wider, within the bound.
A program may use at most 64 MiB of HBM per device.

v0:
```python
import functools

import jax
import jax.numpy as jnp
from jax import lax
from jax.experimental import pallas as pl
from jax.experimental.pallas import tpu as pltpu
from jax.sharding import PartitionSpec as P

F32 = jnp.float32
BF16 = jnp.bfloat16
NT = (((1,), (1,)), ((), ()))
TN = (((0,), (0,)), ((), ()))
HIGH = lax.Precision.HIGHEST


def grid_of(n):
    inner = 1
    while (2 * inner) ** 3 <= n:
        inner *= 2
    return n // (inner * inner), inner, inner


def pack(value):
    rp, dl = value.shape
    q, r = divmod(dl, 128)
    pieces = [value[:, k * 128:(k + 1) * 128] for k in range(q)]
    if r:
        tail = value[:, q * 128:]
        if r <= 64:
            tail = jnp.concatenate([tail, jnp.zeros((rp, 64 - r), tail.dtype)], axis=1) if r < 64 else tail
            tail = jnp.concatenate([tail[:rp // 2], tail[rp // 2:]], axis=1)
        else:
            tail = jnp.concatenate([tail, jnp.zeros((rp, 128 - r), tail.dtype)], axis=1)
        pieces.append(tail)
    return jnp.concatenate(pieces, axis=0) if len(pieces) > 1 else pieces[0]


def unpack(packed, rp, dl):
    q, r = divmod(dl, 128)
    pieces = [packed[k * rp:(k + 1) * rp] for k in range(q)]
    if r:
        tail = packed[q * rp:]
        if r <= 64:
            tail = jnp.concatenate([tail[:, :r], tail[:, 64:64 + r]], axis=0)
        else:
            tail = tail[:, :r]
        pieces.append(tail)
    return jnp.concatenate(pieces, axis=1) if len(pieces) > 1 else pieces[0]


def kernel(
    n, members, lines, rows, width,
    x_in, gain_in, hid_in, cot_in, ids_in, wg_hbm, wu_hbm, emb_hbm, out_ref,
    xg, gg, part, r1y, r1x, r2x, r2y, r3, st_in, st_sq, st_pr, st_cu,
    wg_v, wu_v, wt3, emb_v, emb3, gain3, hcat, acc, inv_ref, sums, kept, scores, others,
    load_sem, st_send, st_recv, x_send, x_recv, g_send, g_recv,
    s1y, q1y, s1x, q1x, s2, q2x, q2y, s3, q3, m_send, m_recv,
):
    A, B, C = lines
    dl = x_in.shape[1]
    rp = hcat.shape[0]
    half = xg.shape[1] // 2
    fl = hid_in.shape[1]
    vl = emb_hbm.shape[0]
    me = lax.axis_index("shard")
    mine = lax.axis_index("member")
    c0 = lax.rem(me, C)
    b0 = lax.rem(lax.div(me, C), B)
    a0 = lax.div(me, B * C)

    def at(a, b, c):
        return (a * B + b) * C + c

    def turn(v, d, size):
        if size & (size - 1):
            return lax.rem(v + d, size)
        for k in range(size.bit_length() - 1):
            bit = 2 ** k
            on = (d // bit) % 2 if isinstance(d, int) else lax.rem(lax.div(d, bit), 2)
            v = v + on * (bit - 2 * bit * lax.rem(lax.div(v, bit), 2))
        return v

    def remote(src, dst, send, recv, peer, axis="shard"):
        return pltpu.make_async_remote_copy(
            src_ref=src, dst_ref=dst, send_sem=send, recv_sem=recv,
            device_id={axis: peer}, device_id_type=pl.DeviceIdType.MESH,
        )

    loads = [
        pltpu.make_async_copy(wg_hbm, wg_v, load_sem.at[0]),
        pltpu.make_async_copy(wu_hbm, wu_v, load_sem.at[1]),
        pltpu.make_async_copy(emb_hbm, emb_v, load_sem.at[2]),
    ]
    for load in loads:
        load.start()

    barrier = pltpu.get_barrier_semaphore()
    for d in range(1, n):
        pl.semaphore_signal(barrier, inc=1, device_id={"shard": turn(me, d, n)},
                            device_id_type=pl.DeviceIdType.MESH)
    for d in range(1, members):
        pl.semaphore_signal(barrier, inc=1, device_id={"member": turn(mine, d, members)},
                            device_id_type=pl.DeviceIdType.MESH)

    pad = jnp.zeros((rp - rows, dl), F32)
    x_own = jnp.concatenate([x_in[...].astype(F32), pad], axis=0)
    xg[me] = pack(x_own).astype(BF16)

    def first_row(k):
        return (lax.broadcasted_iota(jnp.int32, (8, k), 0) == 0).astype(F32)

    def to_row(values):
        return lax.dot_general(first_row(values.shape[1]), values, NT, precision=HIGH,
                               preferred_element_type=F32)[0:1]

    def to_column(row, lanes):
        rows8 = first_row(row.shape[1]) * row
        return lax.dot_general(rows8, jnp.ones((8, lanes), F32), TN, precision=HIGH,
                               preferred_element_type=F32)

    def stat_copy(k, buf, d):
        return remote(st_in.at[k], buf.at[me], st_send.at[k, d], st_recv.at[k, me], turn(me, d, n))

    def stat_send(k, buf):
        for d in range(1, n):
            stat_copy(k, buf, d).start()

    def stat_sum(k, buf):
        total = st_in[k]
        for d in range(1, n):
            src = turn(me, d, n)
            remote(st_in.at[k], buf.at[src], st_send.at[k, d], st_recv.at[k, src], src).wait_recv()
            total = total + buf[src]
        for d in range(1, n):
            stat_copy(k, buf, d).wait_send()
        return total

    st_in[0] = to_row(x_own * x_own)
    for b in range(n):
        gain3[b] = gain_in[:, b * dl:(b + 1) * dl]
    loads[0].wait()
    loads[1].wait()
    for b in range(n):
        wt3[b, 0:fl] = wg_v[:, b * dl:(b + 1) * dl]
        wt3[b, fl:2 * fl] = wu_v[:, b * dl:(b + 1) * dl]
    acc[...] = jnp.zeros_like(acc)
    scores[...] = jnp.zeros_like(scores)
    pl.semaphore_wait(barrier, n - 1 + members - 1)

    def gather(buf, send, recv, before, process, late):
        per = 2 * (B - 1) + 2 * (C - 1) + 2 * (B - 1) * (C - 1)

        def piece(blk, h, index, peer):
            view = buf.at[blk, pl.ds(h * half, half)]
            return remote(view, view, send.at[index], recv.at[blk, h], peer)

        def outs(da):
            a = turn(a0, da, A)
            base = 2 * (A - 1) + da * per
            full, low, high = ([], []), [], []
            k = 0
            for h in (0, 1):
                for dc in range(1, C):
                    full[h].append(piece(at(a, b0, c0), h, base + k, at(a0, b0, turn(c0, dc, C))))
                    k += 1
                for db in range(1, B):
                    full[h].append(piece(at(a, b0, c0), h, base + k, at(a0, turn(b0, db, B), c0)))
                    k += 1
            for dc in range(1, C):
                for db in range(1, B):
                    low.append(piece(at(a, b0, turn(c0, dc, C)), 0, base + k,
                                     at(a0, turn(b0, db, B), c0)))
                    k += 1
            for db in range(1, B):
                for dc in range(1, C):
                    high.append(piece(at(a, turn(b0, db, B), c0), 1, base + k,
                                      at(a0, b0, turn(c0, dc, C))))
                    k += 1
            return full, low, high

        def outer(da, h):
            return piece(me, h, 2 * (da - 1) + h, at(turn(a0, da, A), b0, c0))

        own = outs(0)[0]
        for h in (0, 1):
            for copy in own[h][:C - 1] + own[1 - h][C - 1:]:
                copy.start()
        for da in range(1, A):
            for h in (0, 1):
                outer(da, h).start()

        def step(t, carry):
            @pl.when(jnp.logical_and(t >= 1, t < A))
            def _():
                src = at(turn(a0, t, A), b0, c0)
                full = outs(t)[0]
                for h in (0, 1):
                    piece(src, h, 0, src).wait_recv()
                    for copy in full[h]:
                        copy.start()

            @pl.when(jnp.logical_and(t >= 1, t < A + 1))
            def _():
                a = turn(a0, t - 1, A)
                _, low, high = outs(t - 1)
                for i in range(C - 1):
                    c = turn(c0, i + 1, C)
                    piece(at(a, b0, c), 0, 0, at(a0, b0, c)).wait_recv()
                    for copy in low[i * (B - 1):(i + 1) * (B - 1)]:
                        copy.start()
                for i in range(B - 1):
                    b = turn(b0, i + 1, B)
                    piece(at(a, b, c0), 1, 0, at(a0, b, c0)).wait_recv()
                    for copy in high[i * (C - 1):(i + 1) * (C - 1)]:
                        copy.start()

                @pl.when(t == 1)
                def _():
                    before()

                process(at(a, b0, c0))

            @pl.when(t == A + 1)
            def _():
                late()

            @pl.when(t >= 2)
            def _():
                a = turn(a0, t - 2, A)
                for dc in range(1, C):
                    c = turn(c0, dc, C)
                    piece(at(a, b0, c), 1, 0, at(a0, b0, c)).wait_recv()
                    process(at(a, b0, c))
                for db in range(1, B):
                    b = turn(b0, db, B)
                    piece(at(a, b, c0), 0, 0, at(a0, b, c0)).wait_recv()
                    process(at(a, b, c0))
                for db in range(1, B):
                    for dc in range(1, C):
                        b, c = turn(b0, db, B), turn(c0, dc, C)
                        piece(at(a, b, c), 0, 0, at(a0, b, c0)).wait_recv()
                        piece(at(a, b, c), 1, 0, at(a0, b0, c)).wait_recv()
                        process(at(a, b, c))

            return carry

        lax.fori_loop(0, A + 2, step, 0)

        for da in range(1, A):
            for h in (0, 1):
                outer(da, h).wait_send()

        def done(da, carry):
            full, low, high = outs(da)
            for copy in full[0] + full[1] + low + high:
                copy.wait_send()
            return carry

        lax.fori_loop(0, A, done, 0)

    stat_send(0, st_sq)

    def prepare():
        square = to_column(stat_sum(0, st_sq), 128)
        inv_ref[...] = 1.0 / jnp.sqrt(square / width + 1e-05)

    def up(blk):
        x = unpack(xg[blk].astype(F32), rp, dl)
        normed = (x * inv_ref[:, 0:1] * gain3[blk]).astype(BF16)
        acc[...] += lax.dot_general(normed, wt3[blk], NT, preferred_element_type=F32)

    def table():
        loads[2].wait()
        for b in range(n):
            emb3[b] = emb_v[:, b * dl:(b + 1) * dl]

    gather(xg, x_send, x_recv, prepare, up, table)

    gate_pre = acc[0:rows, 0:fl]
    up_proj = acc[0:rows, fl:2 * fl]
    hid = hid_in[...].astype(F32)
    s = jax.nn.sigmoid(gate_pre)
    gate_grad = (hid * up_proj * s * (1.0 + gate_pre * (1.0 - s))).astype(BF16)
    up_grad = (hid * gate_pre * s).astype(BF16)
    hcat[...] = jnp.zeros_like(hcat)
    hcat[0:rows, 0:fl] = gate_grad
    hcat[0:rows, fl:2 * fl] = up_grad
    st_in[1] = to_row(hcat[...].astype(F32) * acc[...])
    stat_send(1, st_pr)

    def product(blk):
        return pack(jnp.dot(hcat[...], wt3[blk], preferred_element_type=F32))

    lo, hi = pl.ds(0, half), pl.ds(half, half)

    def first(a):
        copies = []
        for db in range(1, B):
            for dc in range(1, C):
                b, c = turn(b0, db, B), turn(c0, dc, C)
                blk = at(a, b, c)
                copies.append((blk, remote(part.at[blk, lo], r1y.at[a, c, b0],
                                           s1y.at[blk], q1y.at[a, c, b0], at(a0, b, c0))))
                copies.append((blk, remote(part.at[blk, hi], r1x.at[a, b, c0],
                                           s1x.at[blk], q1x.at[a, b, c0], at(a0, b0, c))))
        return copies

    def second(a):
        copies = []
        for dc in range(1, C):
            c = turn(c0, dc, C)
            blk = at(a, b0, c)
            pair = [remote(part.at[blk, span], r2x.at[a, c0, span], s2.at[blk, h],
                           q2x.at[a, c0, h], at(a0, b0, c)) for h, span in ((1, hi), (0, lo))]
            copies.append((blk, c, 0, pair))
        for db in range(1, B):
            b = turn(b0, db, B)
            blk = at(a, b, c0)
            pair = [remote(part.at[blk, span], r2y.at[a, b0, span], s2.at[blk, h],
                           q2y.at[a, b0, h], at(a0, b, c0)) for h, span in ((0, lo), (1, hi))]
            copies.append((blk, b, 1, pair))
        return copies

    def third(a, h):
        blk = at(a, b0, c0)
        span = (lo, hi)[h]
        return remote(part.at[blk, span], r3.at[a0, span], s3.at[a, h], q3.at[a0, h], at(a, b0, c0))

    def reduce_step(t, carry):
        @pl.when(t < A)
        def _():
            a = turn(a0, lax.rem(t + 1, A), A)
            for i, (blk, copy) in enumerate(first(a)):
                if i % 2 == 0:
                    part[blk] = product(blk).astype(BF16)
                copy.start()
            for i, (blk, _, way, pair) in enumerate(second(a)):
                value = product(blk)
                if way == 0:
                    part[blk, half:] = value[half:].astype(BF16)
                    kept[lax.rem(t, 2), i] = value[:half]
                else:
                    part[blk, :half] = value[:half].astype(BF16)
                    kept[lax.rem(t, 2), i] = value[half:]
                pair[0].start()

        @pl.when(jnp.logical_and(t >= 1, t < A + 1))
        def _():
            a = turn(a0, lax.rem(t, A), A)
            for i, (blk, other, way, pair) in enumerate(second(a)):
                edge = kept[lax.rem(t - 1, 2), i]
                if way == 0:
                    for db in range(1, B):
                        b = turn(b0, db, B)
                        slot = r1y.at[a, other, b]
                        remote(slot, slot, s1y.at[blk], q1y.at[a, other, b], at(a0, b, c0)).wait_recv()
                        edge = edge + r1y[a, other, b].astype(F32)
                    part[blk, :half] = edge.astype(BF16)
                else:
                    for dc in range(1, C):
                        c = turn(c0, dc, C)
                        slot = r1x.at[a, other, c]
                        remote(slot, slot, s1x.at[blk], q1x.at[a, other, c], at(a0, b0, c)).wait_recv()
                        edge = edge + r1x[a, other, c].astype(F32)
                    part[blk, half:] = edge.astype(BF16)
                pair[1].start()

        @pl.when(t >= 2)
        def _():
            a = turn(a0, t - 1, A) if A & (A - 1) else turn(a0, lax.rem(t - 1, A), A)
            blk = at(a, b0, c0)
            sums[...] = product(blk)
            for h, span in ((0, lo), (1, hi)):
                value = sums[span]
                for dc in range(1, C):
                    c = turn(c0, dc, C)
                    slot = r2x.at[a, c, span]
                    remote(slot, slot, s2.at[blk, h], q2x.at[a, c, h], at(a0, b0, c)).wait_recv()
                    value = value + r2x[a, c, span].astype(F32)
                for db in range(1, B):
                    b = turn(b0, db, B)
                    slot = r2y.at[a, b, span]
                    remote(slot, slot, s2.at[blk, h], q2y.at[a, b, h], at(a0, b, c0)).wait_recv()
                    value = value + r2y[a, b, span].astype(F32)
                sums[span] = value

                @pl.when(t < A + 1)
                def _():
                    part[blk, span] = value.astype(BF16)
                    third(a, h).start()

        return carry

    lax.fori_loop(0, A + 2, reduce_step, 0)

    proj = to_column(stat_sum(1, st_pr), 128)
    share = sums[...]
    for da in range(1, A):
        a = turn(a0, da, A)
        for h, span in ((0, lo), (1, hi)):
            slot = r3.at[a, span]
            remote(slot, slot, s3.at[a, h], q3.at[a, h], at(a, b0, c0)).wait_recv()
        share = share + r3[a].astype(F32)
    inv = inv_ref[:, 0:1]
    scaled = unpack(share, rp, dl) * gain3[me]
    cot = jnp.concatenate([cot_in[...].astype(F32), pad], axis=0)
    grad = cot + inv * scaled - x_own * (inv * inv * (proj[:, 0:1] / width))
    gg[me] = pack(grad).astype(BF16)

    def settle(d, carry):
        a = turn(a0, d, A)
        for _, copy in first(a):
            copy.wait_send()
        for _, _, _, pair in second(a):
            for copy in pair:
                copy.wait_send()

        @pl.when(d >= 1)
        def _():
            third(a, 0).wait_send()
            third(a, 1).wait_send()

        return carry

    def score(blk):
        scores[...] += lax.dot_general(unpack(gg[blk], rp, dl), emb3[blk], NT, preferred_element_type=F32)

    gather(gg, g_send, g_recv, lambda: None, score, lambda: None)
    lax.fori_loop(0, A, settle, 0)

    def member_copy(d):
        return remote(scores, others.at[mine], m_send.at[d], m_recv.at[mine],
                      turn(mine, d, members), "member")

    for d in range(1, members):
        member_copy(d).start()
    ids = to_column(ids_in[...].astype(F32), vl)
    entry = (lax.broadcasted_iota(jnp.int32, (rows, vl), 1) + me * vl).astype(F32)
    total = scores[...]
    for d in range(1, members):
        src = turn(mine, d, members)
        remote(others.at[src], others.at[src], m_send.at[d], m_recv.at[src], src, "member").wait_recv()
        total = total + others[src]
    own = jnp.where(ids == entry, total[0:rows], 0.0)
    st_in[2] = to_row(jnp.concatenate([own, jnp.zeros((rp - rows, vl), F32)], axis=0))
    stat_send(2, st_cu)
    current = to_column(stat_sum(2, st_cu), 128)
    out_ref[...] = total[0:rows] - current[0:rows, 0:1]
    for d in range(1, members):
        member_copy(d).wait_send()


def on_device(n, members, layer_input, norm_gain, w_gate, w_up, hidden_cot, output_cot, embed, suffix_ids):
    _, rows, dl = layer_input.shape
    width = norm_gain.shape[1]
    fl = w_gate.shape[2]
    vl = embed.shape[1]
    lines = A, B, C = grid_of(n)
    rp = -(-rows // 32) * 32
    q, r = divmod(dl, 128)
    length = q * rp + (0 if r == 0 else rp // 2 if r <= 64 else rp)
    half = length // 2
    per = 2 * (B - 1) + 2 * (C - 1) + 2 * (B - 1) * (C - 1)
    moves = 2 * (A - 1) + A * per
    vmem = pl.BlockSpec(memory_space=pltpu.VMEM)
    hbm = pl.BlockSpec(memory_space=pl.ANY)
    dma = pltpu.SemaphoreType.DMA
    V = pltpu.VMEM
    scratch = [
        V((n, length, 128), BF16), V((n, length, 128), BF16), V((n, length, 128), BF16),
        V((A, C, B, half, 128), BF16), V((A, B, C, half, 128), BF16),
        V((A, C, length, 128), BF16), V((A, B, length, 128), BF16), V((A, length, 128), BF16),
        V((3, 1, rp), F32), V((n, 1, rp), F32), V((n, 1, rp), F32), V((n, 1, rp), F32),
        V((fl, width), BF16), V((fl, width), BF16), V((n, 2 * fl, dl), BF16),
        V((vl, width), BF16), V((n, vl, dl), BF16), V((n, 1, dl), F32),
        V((rp, 2 * fl), BF16), V((rp, 2 * fl), F32), V((rp, 128), F32), V((length, 128), F32),
        V((2, B + C - 2, half, 128), F32),
        V((rp, vl), F32), V((members, rp, vl), F32),
        dma((3,)), dma((3, n)), dma((3, n)), dma((moves,)), dma((n, 2)), dma((moves,)), dma((n, 2)),
        dma((n,)), dma((A, C, B)), dma((n,)), dma((A, B, C)), dma((n, 2)), dma((A, C, 2)), dma((A, B, 2)),
        dma((A, 2)), dma((A, 2)), dma((members,)), dma((members,)),
    ]
    return pl.pallas_call(
        functools.partial(kernel, n, members, lines, rows, width),
        out_shape=jax.ShapeDtypeStruct((rows, vl), F32),
        in_specs=[vmem] * 5 + [hbm] * 3,
        out_specs=vmem,
        scratch_shapes=scratch,
        compiler_params=pltpu.CompilerParams(
            collective_id=0, has_side_effects=True, vmem_limit_bytes=56 * 1024 * 1024
        ),
    )(layer_input[0], norm_gain, hidden_cot[0], output_cot[0], suffix_ids[None, :],
      w_gate[0].T, w_up[0].T, embed[0])


def solution(mesh):
    n, members = mesh.shape["shard"], mesh.shape["member"]
    placed = (
        P("member", None, "shard"),
        P("member", None),
        P("member", None, "shard"),
        P("member", None, "shard"),
        P("member", None, "shard"),
        P("member", None, "shard"),
        P("member", "shard", None),
        P(),
    )
    return jax.shard_map(
        functools.partial(on_device, n, members),
        mesh=mesh, in_specs=placed, out_specs=P(None, "shard"), check_vma=False,
    )
```

profile of v0, /device:TPU:0, one launch (start us, length us, event | category | flops | bytes accessed | tf_op | source)
XLA Modules:
  0.0 83.8 jit_solution(16951434833966481651)
XLA Ops:
  0.0 82.2 %shard_map.82 = f32[180,256]{1,0:T(8,128)} custom-call(bf16[180,320]{1,0:T(8,128)(2,1)} %bitcast.14, f32[1,5120]{1,0:T(1,128)} %gain_in.1, bf16[180,112]{1,0:T(8,128)(2,1)} %bitcast.16, bf16[180,320]{1,0:T(8,128)(2,1)} %bitcast.15, s32[1,180]{1,0:T(1,128)} %bitcast.17, bf16[112,5120]{1,0:T(8,128)(2,1)} %bitcast.12, bf16[112,5120]{1,0:T(8,128)(2,1)} %bitcast.13, ...), custom_call_target="tpu_custom_call" | custom-call | tf_op jit(solution)/shard_map/pallas_call | solution.py:484
  82.2 1.6 %copy.10 = f32[180,256]{1,0:T(8,128)} copy(f32[180,256]{1,0:T(8,128)} %shard_map.82) | data formatting | bytes 368640
where the time goes:
time: 84 us; the launch traced here: 83.8 us
  Pallas kernels  82.2 us (98%)
  local copies, waits for them, and re-layouts  1.61 us (2%)
    pallas_call x1, Pallas kernels, on_device(): pl.pallas_call(functools.partial(kernel, n, members, lines, rows, width),...  82.2 us

commit v1 on v0

v1 whole, which is shorter than its diff:
```python
import functools

import jax
import jax.numpy as jnp
from jax import lax
from jax.experimental import pallas as pl
from jax.experimental.pallas import tpu as pltpu
from jax.sharding import PartitionSpec as P

F32 = jnp.float32
BF16 = jnp.bfloat16
NT = (((1,), (1,)), ((), ()))
TN = (((0,), (0,)), ((), ()))
HIGH = lax.Precision.HIGHEST
LAG = 0
PARTS = 1


def grid_of(n):
    inner = 1
    while (2 * inner) ** 3 <= n:
        inner *= 2
    return n // (inner * inner), inner, inner


def ceil_to(v, m):
    return -(-v // m) * m


def fold_of(rp):
    return ceil_to(rp, 16) // 2


def packed_rows(rp, dl):
    q, r = divmod(dl, 128)
    return q * rp + (0 if r == 0 else fold_of(rp) if r <= 64 else rp)


def pack(value):
    rp, dl = value.shape
    q, r = divmod(dl, 128)
    pieces = [value[:, k * 128:(k + 1) * 128] for k in range(q)]
    if r:
        tail = value[:, q * 128:]
        if r <= 64:
            fold = fold_of(rp)
            tail = jnp.concatenate([tail, jnp.zeros((rp, 64 - r), tail.dtype)], axis=1) if r < 64 else tail
            upper = tail[fold:]
            if rp < 2 * fold:
                upper = jnp.concatenate([upper, jnp.zeros((2 * fold - rp, 64), tail.dtype)], axis=0)
            tail = jnp.concatenate([tail[:fold], upper], axis=1)
        else:
            tail = jnp.concatenate([tail, jnp.zeros((rp, 128 - r), tail.dtype)], axis=1)
        pieces.append(tail)
    return jnp.concatenate(pieces, axis=0) if len(pieces) > 1 else pieces[0]


def unpack(packed, rp, dl):
    q, r = divmod(dl, 128)
    pieces = [packed[k * rp:(k + 1) * rp] for k in range(q)]
    if r:
        tail = packed[q * rp:]
        if r <= 64:
            fold = fold_of(rp)
            tail = jnp.concatenate([tail[:, :r], tail[:rp - fold, 64:64 + r]], axis=0)
        else:
            tail = tail[:, :r]
        pieces.append(tail)
    return jnp.concatenate(pieces, axis=1) if len(pieces) > 1 else pieces[0]


def gather_sends(lines):
    A, B, C = lines
    line, diag = B + C - 2, (B - 1) * (C - 1)
    return (A - 1) + 2 * line + 2 * diag + line + (A - 2) * 2 * line + diag + (A - 2) * 2 * diag


CHUNK_BUFFERS = (
    "xg", "gg", "part", "rx", "ry", "rz", "rd", "r1y", "r1x", "st_in", "st_pr", "st_cu",
    "acc", "hcat", "inv", "ssq", "scores", "others", "total",
    "x_send", "x_recv", "g_send", "g_recv", "p_send", "qx", "qy", "qz", "qd", "q1y", "q1x",
    "st_send", "st_recv", "m_send", "m_recv",
)
SHARED = ("wg_v", "wu_v", "wt3", "emb_v", "emb3", "gain3", "idcol", "load_sem")


def kernel(n, members, lines, chunks, width, x_in, gain_in, hid_in, cot_in, ids_in, wg_hbm, wu_hbm, emb_hbm,
           out_ref, *scratch):
    A, B, C = lines
    dl = x_in.shape[1]
    fl = hid_in.shape[1]
    vl = emb_hbm.shape[0]
    rows = x_in.shape[0]
    S = dict(zip(SHARED, scratch))
    scratch = scratch[len(SHARED):]
    K = [dict(zip(CHUNK_BUFFERS, scratch[k * len(CHUNK_BUFFERS):])) for k in range(len(chunks))]
    wt3, emb3, gain3, idcol = S["wt3"], S["emb3"], S["gain3"], S["idcol"]
    flp = wt3.shape[1] // 2
    me = lax.axis_index("shard")
    mine = lax.axis_index("member")
    c0 = lax.rem(me, C)
    b0 = lax.rem(lax.div(me, C), B)
    a0 = lax.div(me, B * C)

    def at(a, b, c):
        return (a * B + b) * C + c

    def turn(v, d, size):
        if size & (size - 1):
            return lax.rem(v + d, size)
        for k in range(size.bit_length() - 1):
            bit = 2 ** k
            on = (d // bit) % 2 if isinstance(d, int) else lax.rem(lax.div(d, bit), 2)
            v = v + on * (bit - 2 * bit * lax.rem(lax.div(v, bit), 2))
        return v

    def remote(src, dst, send, recv, peer, axis="shard"):
        return pltpu.make_async_remote_copy(
            src_ref=src, dst_ref=dst, send_sem=send, recv_sem=recv,
            device_id={axis: peer}, device_id_type=pl.DeviceIdType.MESH,
        )

    plane = [turn(a0, d, A) for d in range(A)]
    xs = [turn(c0, d, C) for d in range(1, C)]
    ys = [turn(b0, d, B) for d in range(1, B)]

    loads = [
        pltpu.make_async_copy(wg_hbm, S["wg_v"], S["load_sem"].at[0]),
        pltpu.make_async_copy(wu_hbm, S["wu_v"], S["load_sem"].at[1]),
        pltpu.make_async_copy(emb_hbm, S["emb_v"], S["load_sem"].at[2]),
    ]
    for load in loads:
        load.start()

    barrier = pltpu.get_barrier_semaphore()
    for d in range(1, n):
        pl.semaphore_signal(barrier, inc=1, device_id={"shard": turn(me, d, n)},
                            device_id_type=pl.DeviceIdType.MESH)
    for d in range(1, members):
        pl.semaphore_signal(barrier, inc=1, device_id={"member": turn(mine, d, members)},
                            device_id_type=pl.DeviceIdType.MESH)

    def first_row(k):
        return (lax.broadcasted_iota(jnp.int32, (8, k), 0) == 0).astype(F32)

    def to_row(values):
        return lax.dot_general(first_row(values.shape[1]), values, NT, precision=HIGH,
                               preferred_element_type=F32)[0:1]

    def to_column(row, lanes):
        rows8 = first_row(row.shape[1]) * row
        return lax.dot_general(rows8, jnp.ones((8, lanes), F32), TN, precision=HIGH,
                               preferred_element_type=F32)

    def pad_rows(value, rp):
        short = rp - value.shape[0]
        return jnp.concatenate([value, jnp.zeros((short, value.shape[1]), value.dtype)], axis=0) if short else value

    waits = []

    def start(copies):
        waits.extend(copies)
        for copy in copies:
            copy.start()

    def halves_of(length):
        low = ceil_to(length // 2, 8)
        return pl.ds(0, low), pl.ds(low, length - low)

    def gather(buf, send, recv, process):
        spans = halves_of(buf.shape[1])
        used = [0]

        def move(blk, h, peer, slot):
            view = buf.at[blk] if h is None else buf.at[blk, spans[h]]
            return remote(view, view, send.at[slot], recv.at[blk, h or 0], peer)

        def piece(blk, h, peer):
            used[0] += 1
            return move(blk, h, peer, used[0] - 1)

        def arrive(blk, h, peer):
            move(blk, h, peer, 0).wait_recv()

        def spread(j):
            blk = at(plane[j], b0, c0)
            if j == 1:
                return [piece(blk, None, at(a0, b0, c)) for c in xs] + [piece(blk, None, at(a0, b, c0)) for b in ys]
            copies = []
            for h in (0, 1):
                copies += [piece(blk, h, at(a0, b0, c)) for c in xs]
                copies += [piece(blk, 1 - h, at(a0, b, c0)) for b in ys]
            return copies

        def cross(j):
            for c in xs:
                arrive(at(plane[j], b0, c), 0, at(a0, b0, c))
                start([piece(at(plane[j], b0, c), 0, at(a0, b, c0)) for b in ys])
            for b in ys:
                arrive(at(plane[j], b, c0), 1, at(a0, b, c0))
                start([piece(at(plane[j], b, c0), 1, at(a0, b0, c)) for c in xs])

        def rest(j):
            for c in xs:
                arrive(at(plane[j], b0, c), 1, at(a0, b0, c))
            for b in ys:
                arrive(at(plane[j], b, c0), 0, at(a0, b, c0))

        def sides(j):
            return [at(plane[j], b0, c) for c in xs] + [at(plane[j], b, c0) for b in ys]

        cells = [(b, c) for b in ys for c in xs]

        def level0():
            start([piece(me, None, at(plane[j], b0, c0)) for j in range(1, A)])
            start(spread(0))

        def level1():
            process([me])
            cross(0)
            for j in range(1, A):
                arrive(at(plane[j], b0, c0), None, at(plane[j], b0, c0))
                start(spread(j))
            rest(0)
            process(sides(0))
            process([at(plane[j], b0, c0) for j in range(1, A)])

        def level2():
            for b, c in cells:
                arrive(at(a0, b, c), 0, at(a0, b, c0))
                arrive(at(a0, b, c), 1, at(a0, b0, c))
                start([piece(at(a0, b, c), None, at(plane[1], b0, c0))])
            for j in range(2, A):
                cross(j)
            process([at(a0, b, c) for b, c in cells])
            for c in xs:
                arrive(at(plane[1], b0, c), None, at(a0, b0, c))
            for b in ys:
                arrive(at(plane[1], b, c0), None, at(a0, b, c0))
            process(sides(1))
            for j in range(2, A):
                rest(j)
                process(sides(j))

        def level3():
            for j in range(2, A):
                for b, c in cells:
                    arrive(at(plane[j], b, c), 0, at(a0, b, c0))
                    arrive(at(plane[j], b, c), 1, at(a0, b0, c))
                process([at(plane[j], b, c) for b, c in cells])
            for b, c in cells:
                arrive(at(plane[1], b, c), None, at(plane[1], b0, c0))
            process([at(plane[1], b, c) for b, c in cells])

        return [level0, level1, level2, level3]

    def program(k):
        r0, real, rp = chunks[k]
        T = K[k]
        length = T["xg"].shape[1]
        lo, hi = halves_of(length)
        part, rx, ry, rz, rd = T["part"], T["rx"], T["ry"], T["rz"], T["rd"]
        st_in, st_send, st_recv = T["st_in"], T["st_send"], T["st_recv"]

        def own_x():
            return pad_rows(x_in[r0:r0 + real].astype(F32), rp)

        def stat_copy(i, buf, d):
            return remote(st_in.at[i], buf.at[me], st_send.at[i, d], st_recv.at[i, me], turn(me, d, n))

        def stat_send(i, buf):
            start([stat_copy(i, buf, d) for d in range(1, n)])

        def stat_sum(i, buf):
            sum_ = st_in[i]
            for d in range(1, n):
                src = turn(me, d, n)
                remote(st_in.at[i], buf.at[src], st_send.at[i, d], st_recv.at[i, src], src).wait_recv()
                sum_ = sum_ + buf[src]
            return sum_

        def up(blocks):
            for blk in blocks:
                raw = T["xg"][blk].astype(F32)
                T["ssq"][...] += raw * raw
                scaled = (unpack(raw, rp, dl) * gain3[blk]).astype(BF16)
                T["acc"][...] += lax.dot_general(scaled, wt3[blk], NT, preferred_element_type=F32)

        def activate():
            square = jnp.sum(unpack(T["ssq"][...], rp, dl), axis=1, keepdims=True)
            inv = 1.0 / jnp.sqrt(square / width + 1e-05)
            T["inv"][...] = jnp.broadcast_to(inv, (rp, 128))
            gate_pre = T["acc"][:, 0:flp] * inv
            up_proj = T["acc"][:, flp:2 * flp] * inv
            hid = pad_rows(hid_in[r0:r0 + real].astype(F32), rp)
            if flp > fl:
                hid = jnp.concatenate([hid, jnp.zeros((rp, flp - fl), F32)], axis=1)
            s = jax.nn.sigmoid(gate_pre)
            gate_grad = (hid * up_proj * s * (1.0 + gate_pre * (1.0 - s))).astype(BF16)
            up_grad = (hid * gate_pre * s).astype(BF16)
            T["hcat"][:, 0:flp] = gate_grad
            T["hcat"][:, flp:2 * flp] = up_grad
            st_in[0] = to_row(gate_grad.astype(F32) * gate_pre + up_grad.astype(F32) * up_proj)
            stat_send(0, T["st_pr"])

        def product(blk):
            return pack(jnp.dot(T["hcat"][...], wt3[blk], preferred_element_type=F32))

        def landed(slot, sem, peer):
            remote(slot, slot, T["p_send"].at[0, 0], sem, peer).wait_recv()
            return slot[...].astype(F32)

        def out(blk, h, span, dst, sem, peer):
            view = part.at[blk] if span is None else part.at[blk, span]
            return remote(view, dst, T["p_send"].at[blk, h], sem, peer)

        cells = [(b, c) for b in ys for c in xs]

        def split(blk, j, b, c):
            start([
                out(blk, 0, lo, T["r1y"].at[plane[j], c, b0, lo], T["q1y"].at[plane[j], c, b0], at(a0, b, c0)),
                out(blk, 1, hi, T["r1x"].at[plane[j], b, c0, hi], T["q1x"].at[plane[j], b, c0], at(a0, b0, c)),
            ])

        def side_sums(j):
            for c in xs:
                blk = at(plane[j], b0, c)
                value = product(blk)
                if j == 1:
                    part[blk] = value.astype(BF16)
                else:
                    edge = value[:lo.size]
                    for b in ys:
                        edge = edge + landed(T["r1y"].at[plane[j], c, b, lo], T["q1y"].at[plane[j], c, b], at(a0, b, c0))
                    part[blk, lo] = edge.astype(BF16)
                    part[blk, hi] = value[lo.size:].astype(BF16)
                start([out(blk, 0, None, rx.at[plane[j], c0], T["qx"].at[plane[j], c0], at(a0, b0, c))])
            for b in ys:
                blk = at(plane[j], b, c0)
                value = product(blk)
                if j == 1:
                    part[blk] = value.astype(BF16)
                else:
                    edge = value[lo.size:]
                    for c in xs:
                        edge = edge + landed(T["r1x"].at[plane[j], b, c, hi], T["q1x"].at[plane[j], b, c], at(a0, b0, c))
                    part[blk, lo] = value[:lo.size].astype(BF16)
                    part[blk, hi] = edge.astype(BF16)
                start([out(blk, 0, None, ry.at[plane[j], b0], T["qy"].at[plane[j], b0], at(a0, b, c0))])

        def column_sum(j):
            value = product(at(plane[j], b0, c0))
            for c in xs:
                value = value + landed(rx.at[plane[j], c], T["qx"].at[plane[j], c], at(a0, b0, c))
            for b in ys:
                value = value + landed(ry.at[plane[j], b], T["qy"].at[plane[j], b], at(a0, b, c0))
            return value

        def reduce0():
            for j in range(2, A):
                for b, c in cells:
                    blk = at(plane[j], b, c)
                    part[blk] = product(blk).astype(BF16)
                    split(blk, j, b, c)
            for b, c in cells:
                blk = at(plane[1], b, c)
                part[blk] = product(blk).astype(BF16)
                start([out(blk, 0, None, rd.at[b, c], T["qd"].at[b, c], at(plane[1], b0, c0))])

        def reduce1():
            side_sums(1)
            for j in range(2, A):
                side_sums(j)
            for b, c in cells:
                blk = at(a0, b, c)
                value = product(blk) + landed(rd.at[b, c], T["qd"].at[b, c], at(plane[1], b0, c0))
                part[blk] = value.astype(BF16)
                split(blk, 0, b, c)

        def reduce2():
            for j in range(1, A):
                blk = at(plane[j], b0, c0)
                part[blk] = column_sum(j).astype(BF16)
                start([out(blk, 0, None, rz.at[a0], T["qz"].at[a0], at(plane[j], b0, c0))])
            side_sums(0)

        def gradient():
            share = column_sum(0)
            for j in range(1, A):
                share = share + landed(rz.at[plane[j]], T["qz"].at[plane[j]], at(plane[j], b0, c0))
            proj = to_column(stat_sum(0, T["st_pr"]), 128)
            inv = T["inv"][:, 0:1]
            scaled = unpack(share, rp, dl) * gain3[me]
            cot = pad_rows(cot_in[r0:r0 + real].astype(F32), rp)
            grad = cot + inv * scaled - own_x() * (inv * inv * (proj[:, 0:1] / width))
            T["gg"][me] = pack(grad).astype(BF16)

        def score(blocks):
            for blk in blocks:
                value = unpack(T["gg"][blk].astype(F32), rp, dl).astype(BF16)
                T["scores"][...] += lax.dot_general(value, emb3[blk], NT, preferred_element_type=F32)

        def member_copy(d):
            return remote(T["scores"], T["others"].at[mine], T["m_send"].at[d], T["m_recv"].at[mine],
                          turn(mine, d, members), "member")

        def exchange():
            start([member_copy(d) for d in range(1, members)])

        def current():
            total = T["scores"][...]
            for d in range(1, members):
                src = turn(mine, d, members)
                slot = T["others"].at[src]
                remote(slot, slot, T["m_send"].at[d], T["m_recv"].at[src], src, "member").wait_recv()
                total = total + slot[...]
            T["total"][...] = total
            entry = (lax.broadcasted_iota(jnp.int32, (rp, vl), 1) + me * vl).astype(F32)
            st_in[1] = to_row(jnp.where(idcol[r0:r0 + rp, 0:1] == entry, total, 0.0))
            stat_send(1, T["st_cu"])

        def finish():
            column = to_column(stat_sum(1, T["st_cu"]), 128)
            out_ref[r0:r0 + real] = (T["total"][...] - column[:, 0:1])[0:real]

        x_stages = gather(T["xg"], T["x_send"], T["x_recv"], up)
        g_stages = gather(T["gg"], T["g_send"], T["g_recv"], score)
        def own_pack():
            T["xg"][me] = pack(own_x()).astype(BF16)

        def clear():
            T["acc"][...] = jnp.zeros_like(T["acc"])
            T["ssq"][...] = jnp.zeros_like(T["ssq"])
            T["scores"][...] = jnp.zeros_like(T["scores"])

        def turn_around():
            gradient()
            g_stages[0]()

        def seq(*stages):
            def stage():
                for part_ in stages:
                    part_()
            return stage

        timed = x_stages[1:3] + [seq(x_stages[3], activate, reduce0), reduce1, reduce2, turn_around]
        timed += g_stages[1:3] + [seq(g_stages[3], exchange), current, finish]
        return own_pack, clear, x_stages[0], timed

    plans = [program(k) for k in range(len(chunks))]
    for own_pack, _, _, _ in plans:
        own_pack()
    pl.semaphore_wait(barrier, n - 1 + members - 1)
    for _, _, begin, _ in plans:
        begin()
    for _, clear, _, _ in plans:
        clear()
    for b in range(n):
        gain3[b] = gain_in[:, b * dl:(b + 1) * dl]
    loads[0].wait()
    loads[1].wait()
    for b in range(n):
        wt3[b, 0:fl] = S["wg_v"][:, b * dl:(b + 1) * dl]
        wt3[b, flp:flp + fl] = S["wu_v"][:, b * dl:(b + 1) * dl]
        if flp > fl:
            wt3[b, fl:flp] = jnp.zeros((flp - fl, dl), BF16)
            wt3[b, flp + fl:] = jnp.zeros((flp - fl, dl), BF16)
    loads[2].wait()
    for b in range(n):
        emb3[b] = S["emb_v"][:, b * dl:(b + 1) * dl]
    ids = to_column(ids_in[...].astype(F32), 128)
    idcol[...] = pad_rows(ids, idcol.shape[0])

    timeline = []
    for k, (_, _, _, timed) in enumerate(plans):
        timeline += [(i + LAG * k, k, stage) for i, stage in enumerate(timed)]
    for _, _, stage in sorted(timeline, key=lambda item: item[:2]):
        stage()
    for copy in waits:
        copy.wait_send()


def split_rows(rows):
    size = ceil_to(-(-rows // PARTS), 16)
    return [(r, min(size, rows - r), ceil_to(min(size, rows - r), 8)) for r in range(0, rows, size)]


def on_device(n, members, layer_input, norm_gain, w_gate, w_up, hidden_cot, output_cot, embed, suffix_ids):
    _, rows, dl = layer_input.shape
    width = norm_gain.shape[1]
    fl = w_gate.shape[2]
    vl = embed.shape[1]
    lines = A, B, C = grid_of(n)
    chunks = split_rows(rows)
    flp = ceil_to(fl, 128)
    sends = gather_sends(lines)
    vmem = pl.BlockSpec(memory_space=pltpu.VMEM)
    hbm = pl.BlockSpec(memory_space=pl.ANY)
    dma = pltpu.SemaphoreType.DMA
    V = pltpu.VMEM
    scratch = [
        V((fl, width), BF16), V((fl, width), BF16), V((n, 2 * flp, dl), BF16),
        V((vl, width), BF16), V((n, vl, dl), BF16), V((n, 1, dl), F32),
        V((chunks[-1][0] + chunks[-1][2], 128), F32), dma((3,)),
    ]
    for _, _, rp in chunks:
        length = packed_rows(rp, dl)
        block = (length, 128)
        scratch += [
            V((n, *block), BF16), V((n, *block), BF16), V((n, *block), BF16),
            V((A, C, *block), BF16), V((A, B, *block), BF16), V((A, *block), BF16), V((B, C, *block), BF16),
            V((A, C, B, *block), BF16), V((A, B, C, *block), BF16),
            V((2, 1, rp), F32), V((n, 1, rp), F32), V((n, 1, rp), F32),
            V((rp, 2 * flp), F32), V((rp, 2 * flp), BF16), V((rp, 128), F32), V(block, F32),
            V((rp, vl), F32), V((members, rp, vl), F32), V((rp, vl), F32),
            dma((sends,)), dma((n, 2)), dma((sends,)), dma((n, 2)), dma((n, 2)),
            dma((A, C)), dma((A, B)), dma((A,)), dma((B, C)), dma((A, C, B)), dma((A, B, C)),
            dma((2, n)), dma((2, n)), dma((members,)), dma((members,)),
        ]
    return pl.pallas_call(
        functools.partial(kernel, n, members, lines, chunks, width),
        out_shape=jax.ShapeDtypeStruct((rows, vl), F32),
        in_specs=[vmem] * 5 + [hbm] * 3,
        out_specs=vmem,
        scratch_shapes=scratch,
        compiler_params=pltpu.CompilerParams(
            collective_id=0, has_side_effects=True, vmem_limit_bytes=60 * 1024 * 1024
        ),
    )(layer_input[0], norm_gain, hidden_cot[0], output_cot[0], suffix_ids[None, :],
      w_gate[0].T, w_up[0].T, embed[0])


def solution(mesh):
    n, members = mesh.shape["shard"], mesh.shape["member"]
    placed = (
        P("member", None, "shard"),
        P("member", None),
        P("member", None, "shard"),
        P("member", None, "shard"),
        P("member", None, "shard"),
        P("member", None, "shard"),
        P("member", "shard", None),
        P(),
    )
    return jax.shard_map(
        functools.partial(on_device, n, members),
        mesh=mesh, in_specs=placed, out_specs=P(None, "shard"), check_vma=False,
    )
```

time: 84 us -> 74 us (0.88)
  Pallas kernels: 82.2 us -> 72.1 us
    pallas_call x1, Pallas kernels: 82.2 us -> 72.1 us  [on_device(): pl.pallas_call(functools.partial(kernel, n, members, lines, chunks, width...]
where the time goes in v1:
time: 74 us; the launch traced here: 73.8 us
  Pallas kernels  72.1 us (97%)
  local copies, waits for them, and re-layouts  1.61 us (2%)
    pallas_call x1, Pallas kernels, on_device(): pl.pallas_call(functools.partial(kernel, n, members, lines, chunks, width...  72.1 us
    unnamed x1, local copies, waits for them, and re-layouts  1.61 us

profile of v1, /device:TPU:0, one launch (start us, length us, event | category | flops | bytes accessed | tf_op | source)
XLA Modules:
  0.0 73.8 jit_solution(9880023220867329847)
XLA Ops:
  0.0 72.1 %shard_map.82 = f32[180,256]{1,0:T(8,128)} custom-call(bf16[180,320]{1,0:T(8,128)(2,1)} %bitcast.14, f32[1,5120]{1,0:T(1,128)} %gain_in.1, bf16[180,112]{1,0:T(8,128)(2,1)} %bitcast.16, bf16[180,320]{1,0:T(8,128)(2,1)} %bitcast.15, s32[1,180]{1,0:T(1,128)} %bitcast.17, bf16[112,5120]{1,0:T(8,128)(2,1)} %bitcast.12, bf16[112,5120]{1,0:T(8,128)(2,1)} %bitcast.13, ...), custom_call_target="tpu_custom_call" | custom-call | tf_op jit(solution)/shard_map/pallas_call | solution.py:520
  72.1 1.6 %copy.10 = f32[180,256]{1,0:T(8,128)} copy(f32[180,256]{1,0:T(8,128)} %shard_map.82) | data formatting | bytes 368640
